TPU v7x, 32 devices: a whole 2x2x4 slice. The times are simulated.
32 devices in a mesh: frame: 8 (over z, y), group: 4 (over x, core).
Axes of the slice: x: 2, y: 2, z: 4, core: 2. Of those that a mesh axis runs over, the one named last changes fastest.
Arguments:
- frames: bfloat16 [32, 64, 1920], P(('frame', 'group')), may hold values from -6 to 6
- motion: int32 [32, 2, 4, 120], P(('frame', 'group')), may hold values from -64 to 64
- weights: int32 [32, 4, 120], P(('frame', 'group')), may hold values from 1 to 16
- strip_map: int32 [32], replicated, may hold values from 0 to 31, each once
- prior_image: float32 [32, 4, 3840], P(('frame', 'group')), may hold values from -6 to 6
- prior_weight: float32 [32, 4, 3840], P(('frame', 'group')), may hold values from 100 to 2000
Outputs:
- joined_image: float32 [32, 4, 3840], P(('frame', 'group'))
Inputs may be any that keep to these rules, and one draw needn't show every extreme that they name: `motion`: motion offsets are whole numbers in high-resolution pixels. `strip_map`: each strip number appears exactly once.
All inputs are finite; a program needn't handle non-finite values.
Results may differ from a plain program's by a relative error of at most 0.0003.
Values sent between devices are 32-bit elements; how exact they have to be, the bound alone decides.
A program may use at most 256 MiB of HBM per device.

v0:
```python
import functools

import jax
import jax.numpy as jnp
from jax import lax
from jax.experimental import pallas as pl
from jax.experimental.pallas import tpu as pltpu
from jax.sharding import PartitionSpec as P

MAX_SHIFT = 64
BLOCK = 32
LANES = 128
MESH = pl.DeviceIdType.MESH


def part_plan(devices, tiles):
    bits = devices.bit_length() - 1
    rest = list(range(1, bits))
    count = 3
    cuts = [tiles * q // count for q in range(count + 1)]
    return [
        (cuts[q], cuts[q + 1], [0] + rest[q:] + rest[:q])
        for q in range(count)
    ]


def splat_kernel(plan, strip_rows, map_ref, motion_ref, weight_ref, frame_ref, *refs):
    outs = refs[: len(plan)]
    rows_ref, up_ref, val_a, val_b, cnt_a, cnt_b = refs[len(plan):]
    low_rows, low_cols = frame_ref.shape[1:]
    grid_rows = 2 * low_rows
    bands = grid_rows // BLOCK
    strips = map_ref.shape[0]
    for acc in (val_a, val_b, cnt_a, cnt_b):
        def clear(t, carry, acc=acc):
            acc[t] = jnp.zeros(acc.shape[1:], jnp.float32)
            return carry
        lax.fori_loop(0, acc.shape[0], clear, 0)

    r = lax.broadcasted_iota(jnp.int32, (grid_rows, low_rows), 0)
    k = lax.broadcasted_iota(jnp.int32, (grid_rows, low_rows), 1)
    own = r // 2
    near = jnp.clip(own - 1 + 2 * (r % 2), 0, low_rows - 1)
    select = jnp.concatenate([(k == own).astype(jnp.float32), (k == near).astype(jnp.float32)], axis=0)
    picked = jnp.dot(select.astype(jnp.bfloat16), frame_ref[0], preferred_element_type=jnp.float32)
    rows_ref[:, LANES : LANES + low_cols] = picked.astype(jnp.bfloat16)
    rows_ref[:, :LANES] = jnp.broadcast_to(picked[:, :1], (2 * grid_rows, LANES)).astype(jnp.bfloat16)
    rows_ref[:, LANES + low_cols :] = jnp.broadcast_to(
        picked[:, low_cols - 1 :], (2 * grid_rows, LANES)
    ).astype(jnp.bfloat16)
    kk = lax.broadcasted_iota(jnp.int32, (3 * LANES, 2 * LANES), 0)
    nn = lax.broadcasted_iota(jnp.int32, (3 * LANES, 2 * LANES), 1)
    mid = nn // 2 + LANES
    spread = jnp.where(kk == mid, 0.75, jnp.where(kk == mid - 1 + 2 * (nn % 2), 0.25, 0.0)).astype(jnp.bfloat16)
    lane = lax.broadcasted_iota(jnp.int32, (BLOCK, LANES), 1)

    def low_tile(u, carry):
        z = jnp.dot(
            rows_ref[:, pl.ds(pl.multiple_of(u * LANES, LANES), 3 * LANES)], spread,
            preferred_element_type=jnp.float32,
        )
        up_ref[...] = 0.75 * z[:grid_rows] + 0.25 * z[grid_rows:]
        for half in range(2):
            for j in range(LANES // BLOCK):
                for b in range(bands):
                    column = u * (2 * LANES // BLOCK) + half * (LANES // BLOCK) + j
                    dy = motion_ref[0, 0, b, column]
                    dx = motion_ref[0, 1, b, column]
                    w = weight_ref[0, b, column].astype(jnp.float32)
                    place = LANES + column * BLOCK + dx
                    tile = place // LANES
                    start = place % LANES
                    top = MAX_SHIFT + b * BLOCK + dy
                    block = up_ref[b * BLOCK : (b + 1) * BLOCK, half * LANES : (half + 1) * LANES]
                    block = pltpu.roll(block, (dx + LANES) % LANES, 1) * w
                    in_a = (lane >= start) & (lane < start + BLOCK)
                    in_b = lane < start + BLOCK - LANES
                    at = pl.ds(top, BLOCK)
                    val_a[tile, at, :] += jnp.where(in_a, block, 0.0)
                    val_b[tile + 1, at, :] += jnp.where(in_b, block, 0.0)
                    cnt_a[tile, at, :] += jnp.where(in_a, w, 0.0)
                    cnt_b[tile + 1, at, :] += jnp.where(in_b, w, 0.0)
        return carry

    lax.fori_loop(0, low_cols // LANES, low_tile, 0)

    def strip(s, carry):
        at = pl.ds(MAX_SHIFT + map_ref[s] * strip_rows, strip_rows)
        for (low, high, order), out in zip(plan, outs):
            position = 0
            for bit in order:
                position = position * 2 + (s // 2**bit) % 2
            for t in range(low, high):
                row = (t - low) * strip_rows
                out[position, row : row + strip_rows, :] = val_a[t + 1, at, :] + val_b[t + 1, at, :]
                row += (high - low) * strip_rows
                out[position, row : row + strip_rows, :] = cnt_a[t + 1, at, :] + cnt_b[t + 1, at, :]
        return carry

    lax.fori_loop(0, strips, strip, 0)


def join_kernel(plan, group_size, image_ref, prior_ref, *refs):
    count = len(plan)
    bits = len(plan[0][2])
    parts = refs[:count]
    out_ref = refs[count]
    landed = refs[count + 1 : count + 1 + count * bits]
    send_sem, recv_sem = refs[-2:]
    strip_rows = out_ref.shape[1]
    me = lax.axis_index("frame") * group_size + lax.axis_index("group")

    def partner(bit):
        other = me + 2**bit - 2 * 2**bit * ((me // 2**bit) % 2)
        return (other // group_size, other % group_size)

    barrier = pltpu.get_barrier_semaphore()
    for bit in range(bits):
        pl.semaphore_signal(barrier, inc=1, device_id=partner(bit), device_id_type=MESH)
    pl.semaphore_wait(barrier, bits)

    def source_of(q, stage):
        return parts[q] if stage == 0 else landed[q * bits + stage - 1]

    def copy_of(q, stage):
        source = source_of(q, stage)
        half = source.shape[0] // 2
        bit = plan[q][2][stage]
        mine = (me // 2**bit) % 2
        return pltpu.make_async_remote_copy(
            src_ref=source.at[pl.ds((1 - mine) * half, half)],
            dst_ref=landed[q * bits + stage],
            send_sem=send_sem.at[q, stage],
            recv_sem=recv_sem.at[q, stage],
            device_id=partner(bit),
            device_id_type=MESH,
        )

    copies = {}
    for q in range(count):
        copies[q, 0] = copy_of(q, 0)
        copies[q, 0].start()
    for stage in range(bits):
        for q in range(count):
            copies[q, stage].wait_recv()
            source = source_of(q, stage)
            half = source.shape[0] // 2
            mine = (me // 2 ** plan[q][2][stage]) % 2
            dest = landed[q * bits + stage]

            for i in range(half):
                dest[i] = dest[i] + source[mine * half + i]
            if stage + 1 < bits:
                copies[q, stage + 1] = copy_of(q, stage + 1)
                copies[q, stage + 1].start()
    for q, (low, high, _) in enumerate(plan):
        total = landed[q * bits + bits - 1]
        for t in range(low, high):
            row = (t - low) * strip_rows
            weighted = total[0, row : row + strip_rows, :]
            row += (high - low) * strip_rows
            counts = total[0, row : row + strip_rows, :]
            cols = slice(t * LANES, (t + 1) * LANES)
            prior = prior_ref[0, :, cols]
            out_ref[0, :, cols] = (weighted + prior * image_ref[0, :, cols]) / (counts + prior)
    for copy in copies.values():
        copy.wait_send()


def body(group_size, frames, motion, weights, strip_map, prior_image, prior_weight):
    low_rows, low_cols = frames.shape[1:]
    strips = strip_map.shape[0]
    strip_rows = prior_image.shape[1]
    tiles = 2 * low_cols // LANES
    plan = part_plan(strips, tiles)
    bits = len(plan[0][2])
    vmem = pl.BlockSpec(memory_space=pltpu.VMEM)
    smem = pl.BlockSpec(memory_space=pltpu.SMEM)
    sizes = [2 * (high - low) * strip_rows for low, high, _ in plan]
    acc = pltpu.VMEM((tiles + 3, 2 * low_rows + 2 * MAX_SHIFT, LANES), jnp.float32)
    parts = pl.pallas_call(
        functools.partial(splat_kernel, plan, strip_rows),
        out_shape=[jax.ShapeDtypeStruct((strips, size, LANES), jnp.float32) for size in sizes],
        in_specs=[smem, smem, smem, vmem],
        out_specs=[vmem] * len(plan),
        scratch_shapes=[
            pltpu.VMEM((4 * low_rows, low_cols + 2 * LANES), jnp.bfloat16),
            pltpu.VMEM((2 * low_rows, 2 * LANES), jnp.float32),
            acc, acc, acc, acc,
        ],
        name="splat",
    )(strip_map, motion, weights, frames)
    landed = [
        pltpu.VMEM((strips >> (stage + 1), size, LANES), jnp.float32)
        for size in sizes for stage in range(bits)
    ]
    return pl.pallas_call(
        functools.partial(join_kernel, plan, group_size),
        out_shape=jax.ShapeDtypeStruct(prior_image.shape, jnp.float32),
        in_specs=[vmem] * (2 + len(plan)),
        out_specs=vmem,
        scratch_shapes=landed + [
            pltpu.SemaphoreType.DMA((len(plan), bits)),
            pltpu.SemaphoreType.DMA((len(plan), bits)),
        ],
        compiler_params=pltpu.CompilerParams(collective_id=0, has_side_effects=True),
        name="join",
    )(prior_image, prior_weight, *parts)


def solution(mesh):
    in_specs = (
        P(("frame", "group"), None, None),
        P(("frame", "group"), None, None, None),
        P(("frame", "group"), None, None),
        P(),
        P(("frame", "group"), None, None),
        P(("frame", "group"), None, None),
    )
    out_specs = P(("frame", "group"), None, None)
    return jax.shard_map(
        functools.partial(body, mesh.shape["group"]), mesh=mesh, in_specs=in_specs, out_specs=out_specs,
        check_vma=False,
    )
```

profile of v0, /device:TPU:0, one launch (start us, length us, event | category | flops | bytes accessed | tf_op | source)
XLA Modules:
  0.0 56.0 jit_solution(14180174318484918857)
XLA Ops:
  0.0 16.4 %splat.1 = (f32[32,80,128]{2,1,0:T(8,128)}, f32[32,80,128]{2,1,0:T(8,128)}, f32[32,80,128]{2,1,0:T(8,128)}) custom-call(s32[32]{0:T(128)} %map_ref.1, s32[1,2,4,120]{3,2,1,0:T(4,128)} %motion_ref.1, s32[1,4,120]{2,1,0:T(4,128)} %weight_ref.1, bf16[1,64,1920]{2,1,0:T(8,128)(2,1)} %frame_ref.1), custom_call_target="tpu_custom_call" | custom-call | tf_op jit(solution)/shard_map/splat/pallas_call | solution.py:181
  16.4 38.1 %join.1 = f32[1,4,3840]{2,1,0:T(4,128)} custom-call(f32[1,4,3840]{2,1,0:T(4,128)} %image_ref.1, f32[1,4,3840]{2,1,0:T(4,128)} %prior_ref.1, f32[32,80,128]{2,1,0:T(8,128)} %get-tuple-element.8.refs_0_, f32[32,80,128]{2,1,0:T(8,128)} %get-tuple-element.9.refs_1_, f32[32,80,128]{2,1,0:T(8,128)} %get-tuple-element.10.refs_2_), custom_call_target="tpu_custom_call" | custom-call | tf_op jit(solution)/shard_map/join/pallas_call | solution.py:197
  54.5 1.5 %copy.8 = f32[1,4,3840]{2,1,0:T(4,128)} copy(f32[1,4,3840]{2,1,0:T(4,128)} %join.1) | data formatting | bytes 122880
where the time goes:
time: 56.2 us; the launch traced here: 56 us
  Pallas kernels  54.5 us (97%)
  local copies, waits for them, and re-layouts  1.46 us (3%)
    pallas_call x1, Pallas kernels, body(): pl.pallas_call(functools.partial(join_kernel, plan, group_size), out_shap...  38.1 us
    pallas_call x1, Pallas kernels, body(): pl.pallas_call(functools.partial(splat_kernel, plan, strip_rows), out_sha...  16.4 us
    unnamed x1, local copies, waits for them, and re-layouts  1.46 us

commit v1 on v0

--- a/solution.py
+++ b/solution.py
@@ -8,6 +8,7 @@
 from jax.sharding import PartitionSpec as P
 
 MAX_SHIFT = 64
+SIDE = 2
 BLOCK = 32
 LANES = 128
 MESH = pl.DeviceIdType.MESH
@@ -15,23 +16,35 @@
 
 def part_plan(devices, tiles):
     bits = devices.bit_length() - 1
-    rest = list(range(1, bits))
+    rest = list(range(1, bits - 1))
     count = 3
-    cuts = [tiles * q // count for q in range(count + 1)]
-    return [
-        (cuts[q], cuts[q + 1], [0] + rest[q:] + rest[:q])
-        for q in range(count)
-    ]
-
-
-def splat_kernel(plan, strip_rows, map_ref, motion_ref, weight_ref, frame_ref, *refs):
+    plan = [[], []]
+    for q in range(count):
+        low, high = tiles * q // count, tiles * (q + 1) // count
+        middle = min(high, low + ((high - low + 1) // 2 + 1) // 2 * 2)
+        turn = q % len(rest)
+        order = [0] + rest[turn:] + rest[:turn] + [bits - 1]
+        plan[0].append((low, middle, order))
+        plan[1].append((middle, high, order))
+    return plan[0] + plan[1]
+
+
+def splat_kernel(
+    plan, strip_rows, map_ref, motion_ref, weight_ref, frame_ref, moves_ref, scores_ref, table_ref, *refs
+):
     outs = refs[: len(plan)]
-    rows_ref, up_ref, val_a, val_b, cnt_a, cnt_b = refs[len(plan):]
+    rows_ref, up_ref, val_a, val_b = refs[len(plan):]
     low_rows, low_cols = frame_ref.shape[1:]
     grid_rows = 2 * low_rows
     bands = grid_rows // BLOCK
     strips = map_ref.shape[0]
-    for acc in (val_a, val_b, cnt_a, cnt_b):
+    block_count = moves_ref.shape[3]
+    table_ref[...] = jnp.zeros(table_ref.shape, jnp.int32)
+    table_ref[:bands, :block_count] = moves_ref[0, 1]
+    table_ref[bands : 2 * bands, :block_count] = moves_ref[0, 0]
+    table_ref[2 * bands : 3 * bands, :block_count] = scores_ref[0]
+    table_ref[...] = pltpu.roll(table_ref[...], SIDE, 1)
+    for acc in (val_a, val_b):
         def clear(t, carry, acc=acc):
             acc[t] = jnp.zeros(acc.shape[1:], jnp.float32)
             return carry
@@ -68,18 +81,16 @@
                     dx = motion_ref[0, 1, b, column]
                     w = weight_ref[0, b, column].astype(jnp.float32)
                     place = LANES + column * BLOCK + dx
-                    tile = place // LANES
-                    start = place % LANES
+                    tile = place >> 7
+                    start = place & (LANES - 1)
                     top = MAX_SHIFT + b * BLOCK + dy
                     block = up_ref[b * BLOCK : (b + 1) * BLOCK, half * LANES : (half + 1) * LANES]
-                    block = pltpu.roll(block, (dx + LANES) % LANES, 1) * w
+                    block = pltpu.roll(block, dx & (LANES - 1), 1) * w
                     in_a = (lane >= start) & (lane < start + BLOCK)
                     in_b = lane < start + BLOCK - LANES
                     at = pl.ds(top, BLOCK)
                     val_a[tile, at, :] += jnp.where(in_a, block, 0.0)
                     val_b[tile + 1, at, :] += jnp.where(in_b, block, 0.0)
-                    cnt_a[tile, at, :] += jnp.where(in_a, w, 0.0)
-                    cnt_b[tile + 1, at, :] += jnp.where(in_b, w, 0.0)
         return carry
 
     lax.fori_loop(0, low_cols // LANES, low_tile, 0)
@@ -89,29 +100,36 @@
         for (low, high, order), out in zip(plan, outs):
             position = 0
             for bit in order:
-                position = position * 2 + (s // 2**bit) % 2
+                position = position * 2 + ((s >> bit) & 1)
             for t in range(low, high):
                 row = (t - low) * strip_rows
                 out[position, row : row + strip_rows, :] = val_a[t + 1, at, :] + val_b[t + 1, at, :]
-                row += (high - low) * strip_rows
-                out[position, row : row + strip_rows, :] = cnt_a[t + 1, at, :] + cnt_b[t + 1, at, :]
         return carry
 
     lax.fori_loop(0, strips, strip, 0)
 
 
-def join_kernel(plan, group_size, image_ref, prior_ref, *refs):
+def join_kernel(plan, group_size, map_ref, table_ref, image_ref, prior_ref, *refs):
     count = len(plan)
     bits = len(plan[0][2])
     parts = refs[:count]
     out_ref = refs[count]
     landed = refs[count + 1 : count + 1 + count * bits]
-    send_sem, recv_sem = refs[-2:]
+    gathered, staged, move_x, move_y, weight, counts, send_sem, recv_sem, table_send, table_recv = refs[
+        count + 1 + count * bits :
+    ]
     strip_rows = out_ref.shape[1]
+    tiles = out_ref.shape[2] // LANES
+    devices = gathered.shape[0]
+    blocks = staged.shape[1]
+    bands = blocks // devices
     me = lax.axis_index("frame") * group_size + lax.axis_index("group")
 
+    def bit_of(bit):
+        return (me // 2**bit) % 2
+
     def partner(bit):
-        other = me + 2**bit - 2 * 2**bit * ((me // 2**bit) % 2)
+        other = me + 2**bit - 2 * 2**bit * bit_of(bit)
         return (other // group_size, other % group_size)
 
     barrier = pltpu.get_barrier_semaphore()
@@ -126,9 +144,8 @@
         source = source_of(q, stage)
         half = source.shape[0] // 2
         bit = plan[q][2][stage]
-        mine = (me // 2**bit) % 2
         return pltpu.make_async_remote_copy(
-            src_ref=source.at[pl.ds((1 - mine) * half, half)],
+            src_ref=source.at[pl.ds((1 - bit_of(bit)) * half, half)],
             dst_ref=landed[q * bits + stage],
             send_sem=send_sem.at[q, stage],
             recv_sem=recv_sem.at[q, stage],
@@ -136,34 +153,94 @@
             device_id_type=MESH,
         )
 
+    slot = 0
+    for step in range(bits):
+        slot = slot + bit_of(bits - 1 - step) * 2**step
+
+    def table_copy(step):
+        size = 2**step
+        window = pl.ds(slot // size * size, size)
+        return pltpu.make_async_remote_copy(
+            src_ref=table_ref if step == 0 else gathered.at[window],
+            dst_ref=gathered.at[slot] if step == 0 else gathered.at[window],
+            send_sem=table_send.at[step],
+            recv_sem=table_recv.at[step],
+            device_id=partner(bits - 1 - step),
+            device_id_type=MESH,
+        )
+
+    def turn_tables():
+        for f in range(devices):
+            for c in range(3):
+                staged[c, f * bands : (f + 1) * bands, :] = gathered[f, c * bands : (c + 1) * bands, :]
+        for low in range(0, blocks, LANES):
+            high = min(blocks, low + LANES)
+            for c, dest in enumerate((move_x, move_y, weight)):
+                dest[:, low:high] = jnp.transpose(staged[c, low:high, :].astype(jnp.float32)).astype(dest.dtype)
+
+    def count_tiles(first, last):
+        position = map_ref[me] * strip_rows + lax.broadcasted_iota(jnp.int32, (8, blocks), 0)
+        position = position - BLOCK * (lax.broadcasted_iota(jnp.int32, (8, blocks), 1) % bands)
+        column = lax.broadcasted_iota(jnp.int32, (LANES, blocks), 0)
+        per_tile = LANES // BLOCK
+
+        def tile(t, carry):
+            total = jnp.zeros((8, LANES), jnp.float32)
+            for i in range(per_tile + 2 * SIDE):
+                at = pl.ds(per_tile * t + i, 1)
+                rows_in = ((position - move_y[at, :]) & -BLOCK) == 0
+                cols_in = ((column - (move_x[at, :] + BLOCK * (i - SIDE))) & -BLOCK) == 0
+                total = total + lax.dot_general(
+                    jnp.where(rows_in, weight[at, :], 0.0).astype(jnp.bfloat16),
+                    jnp.where(cols_in, 1.0, 0.0).astype(jnp.bfloat16),
+                    (((1,), (1,)), ((), ())),
+                    preferred_element_type=jnp.float32,
+                )
+            counts[t] = total
+            return carry
+
+        lax.fori_loop(first, last, tile, 0)
+
     copies = {}
+    table_copies = [table_copy(step) for step in range(bits)]
+    table_copies[0].start()
     for q in range(count):
         copies[q, 0] = copy_of(q, 0)
         copies[q, 0].start()
+    gathered[slot] = table_ref[...]
+    count_slots = list(range(bits, 2 * bits - 1))
     for stage in range(bits):
-        for q in range(count):
-            copies[q, stage].wait_recv()
-            source = source_of(q, stage)
-            half = source.shape[0] // 2
-            mine = (me // 2 ** plan[q][2][stage]) % 2
-            dest = landed[q * bits + stage]
-
-            for i in range(half):
-                dest[i] = dest[i] + source[mine * half + i]
-            if stage + 1 < bits:
-                copies[q, stage + 1] = copy_of(q, stage + 1)
-                copies[q, stage + 1].start()
+        for chunk in range(2):
+            for q in range(chunk * count // 2, (chunk + 1) * count // 2):
+                copies[q, stage].wait_recv()
+                source = source_of(q, stage)
+                half = source.shape[0] // 2
+                mine = bit_of(plan[q][2][stage])
+                dest = landed[q * bits + stage]
+                dest[...] = dest[...] + source[pl.ds(mine * half, half)]
+                if stage + 1 < bits:
+                    copies[q, stage + 1] = copy_of(q, stage + 1)
+                    copies[q, stage + 1].start()
+            at = 2 * stage + chunk
+            step = at - 1
+            if 0 <= step < bits:
+                table_copies[step].wait_recv()
+                if step + 1 < bits:
+                    table_copies[step + 1].start()
+                else:
+                    turn_tables()
+            if at in count_slots:
+                n = count_slots.index(at)
+                count_tiles(tiles * n // len(count_slots), tiles * (n + 1) // len(count_slots))
     for q, (low, high, _) in enumerate(plan):
         total = landed[q * bits + bits - 1]
         for t in range(low, high):
             row = (t - low) * strip_rows
             weighted = total[0, row : row + strip_rows, :]
-            row += (high - low) * strip_rows
-            counts = total[0, row : row + strip_rows, :]
             cols = slice(t * LANES, (t + 1) * LANES)
             prior = prior_ref[0, :, cols]
-            out_ref[0, :, cols] = (weighted + prior * image_ref[0, :, cols]) / (counts + prior)
-    for copy in copies.values():
+            out_ref[0, :, cols] = (weighted + prior * image_ref[0, :, cols]) / (counts[t, :strip_rows, :] + prior)
+    for copy in list(copies.values()) + table_copies:
         copy.wait_send()
 
 
@@ -176,20 +253,25 @@
     bits = len(plan[0][2])
     vmem = pl.BlockSpec(memory_space=pltpu.VMEM)
     smem = pl.BlockSpec(memory_space=pltpu.SMEM)
-    sizes = [2 * (high - low) * strip_rows for low, high, _ in plan]
+    sizes = [(high - low) * strip_rows for low, high, _ in plan]
     acc = pltpu.VMEM((tiles + 3, 2 * low_rows + 2 * MAX_SHIFT, LANES), jnp.float32)
-    parts = pl.pallas_call(
+    bands = motion.shape[2]
+    width = -(-(motion.shape[3] + 2 * SIDE) // LANES) * LANES
+    table_rows = -(-3 * bands // 8) * 8
+    blocks = strips * bands
+    table, *parts = pl.pallas_call(
         functools.partial(splat_kernel, plan, strip_rows),
-        out_shape=[jax.ShapeDtypeStruct((strips, size, LANES), jnp.float32) for size in sizes],
-        in_specs=[smem, smem, smem, vmem],
-        out_specs=[vmem] * len(plan),
+        out_shape=[jax.ShapeDtypeStruct((table_rows, width), jnp.int32)]
+        + [jax.ShapeDtypeStruct((strips, size, LANES), jnp.float32) for size in sizes],
+        in_specs=[smem, smem, smem, vmem, vmem, vmem],
+        out_specs=[vmem] * (1 + len(plan)),
         scratch_shapes=[
             pltpu.VMEM((4 * low_rows, low_cols + 2 * LANES), jnp.bfloat16),
             pltpu.VMEM((2 * low_rows, 2 * LANES), jnp.float32),
-            acc, acc, acc, acc,
+            acc, acc,
         ],
         name="splat",
-    )(strip_map, motion, weights, frames)
+    )(strip_map, motion, weights, frames, motion, weights)
     landed = [
         pltpu.VMEM((strips >> (stage + 1), size, LANES), jnp.float32)
         for size in sizes for stage in range(bits)
@@ -197,15 +279,23 @@
     return pl.pallas_call(
         functools.partial(join_kernel, plan, group_size),
         out_shape=jax.ShapeDtypeStruct(prior_image.shape, jnp.float32),
-        in_specs=[vmem] * (2 + len(plan)),
+        in_specs=[smem] + [vmem] * (3 + len(plan)),
         out_specs=vmem,
         scratch_shapes=landed + [
+            pltpu.VMEM((strips, table_rows, width), jnp.int32),
+            pltpu.VMEM((3, blocks, width), jnp.int32),
+            pltpu.VMEM((width, blocks), jnp.int32),
+            pltpu.VMEM((width, blocks), jnp.int32),
+            pltpu.VMEM((width, blocks), jnp.float32),
+            pltpu.VMEM((tiles, 8, LANES), jnp.float32),
             pltpu.SemaphoreType.DMA((len(plan), bits)),
             pltpu.SemaphoreType.DMA((len(plan), bits)),
+            pltpu.SemaphoreType.DMA((bits,)),
+            pltpu.SemaphoreType.DMA((bits,)),
         ],
         compiler_params=pltpu.CompilerParams(collective_id=0, has_side_effects=True),
         name="join",
-    )(prior_image, prior_weight, *parts)
+    )(strip_map, table, prior_image, prior_weight, *parts)
 
 
 def solution(mesh):

time: 56.2 us -> 45.1 us (0.80)
  the two profiles are of different devices: /device:TPU:0 before, /device:TPU:1 now
where the time goes in v1:
time: 45.1 us; the launch traced here: 44.8 us
  Pallas kernels  43.3 us (96%)
  local copies, waits for them, and re-layouts  1.46 us (3%)
    pallas_call x1, Pallas kernels, body(): pl.pallas_call(functools.partial(join_kernel, plan, group_size), out_shap...  31.4 us
    pallas_call x1, Pallas kernels, body(): pl.pallas_call(functools.partial(splat_kernel, plan, strip_rows), out_sha...  12 us
    unnamed x1, local copies, waits for them, and re-layouts  1.46 us

profile of v1, /device:TPU:1, one launch (start us, length us, event | category | flops | bytes accessed | tf_op | source)
XLA Modules:
  0.0 44.8 jit_solution(7804696529315365700)
XLA Ops:
  0.0 12.0 %splat.1 = (s32[16,128]{1,0:T(8,128)}, f32[32,24,128]{2,1,0:T(8,128)}, f32[32,24,128]{2,1,0:T(8,128)}, f32[32,24,128]{2,1,0:T(8,128)}, f32[32,16,128]{2,1,0:T(8,...) custom-call(s32[32]{0:T(128)} %map_ref.3, s32[1,2,4,120]{3,2,1,0:T(4,128)} %moves_ref.1, s32[1,4,120]{2,1,0:T(4,128)} %scores_ref.1, ...), custom_call_target="tpu_custom_call" | custom-call | tf_op jit(solution)/shard_map/splat/pallas_call | solution.py:262
  12.0 31.4 %join.1 = f32[1,4,3840]{2,1,0:T(4,128)} custom-call(s32[32]{0:T(128)} %map_ref.3, s32[16,128]{1,0:T(8,128)} %get-tuple-element.12.table_ref, f32[1,4,3840]{2,1,0:T(4,128)} %image_ref.1, f32[1,4,3840]{2,1,0:T(4,128)} %prior_ref.1, f32[32,24,128]{2,1,0:T(8,128)} %get-tuple-element.13.refs_0_, f32[32,24,128]{2,1,0:T(8,128)} %get-tuple-element.14.refs_1_, ...), custom_call_target="tpu_custom_call" | custom-call | tf_op jit(solution)/shard_map/join/pallas_call | solution.py:279
  43.3 1.5 %copy.8 = f32[1,4,3840]{2,1,0:T(4,128)} copy(f32[1,4,3840]{2,1,0:T(4,128)} %join.1) | data formatting | bytes 122880

commit v2 on v1

--- a/solution.py
+++ b/solution.py
@@ -29,42 +29,43 @@
     return plan[0] + plan[1]
 
 
-def splat_kernel(
-    plan, strip_rows, map_ref, motion_ref, weight_ref, frame_ref, moves_ref, scores_ref, table_ref, *refs
-):
+def splat_kernel(plan, strip_rows, map_hbm, motion_hbm, weight_hbm, frame_hbm, table_ref, *refs):
     outs = refs[: len(plan)]
-    rows_ref, up_ref, val_a, val_b = refs[len(plan):]
-    low_rows, low_cols = frame_ref.shape[1:]
+    map_ref, motion_ref, weight_ref, moves_ref, scores_ref, rows_ref, up_ref, val_a, val_b, sems = refs[len(plan):]
+    low_rows, low_cols = frame_hbm.shape[1:]
     grid_rows = 2 * low_rows
     bands = grid_rows // BLOCK
     strips = map_ref.shape[0]
+    moved = [
+        (frame_hbm.at[0], rows_ref.at[:, LANES : LANES + low_cols]),
+        (motion_hbm, moves_ref), (weight_hbm, scores_ref),
+        (motion_hbm, motion_ref), (weight_hbm, weight_ref), (map_hbm, map_ref),
+    ]
+    moved = [pltpu.make_async_copy(x, y, sems.at[n]) for n, (x, y) in enumerate(moved)]
+    for copy in moved:
+        copy.start()
+    for acc in (val_a, val_b):
+        def clear(t, carry, acc=acc):
+            acc[t] = jnp.zeros(acc.shape[1:], jnp.float32)
+            return carry
+        lax.fori_loop(0, acc.shape[0], clear, 0)
+    kk = lax.broadcasted_iota(jnp.int32, (3 * LANES, 2 * LANES), 0)
+    nn = lax.broadcasted_iota(jnp.int32, (3 * LANES, 2 * LANES), 1)
+    mid = (nn >> 1) + LANES
+    spread = jnp.where(kk == mid, 0.75, jnp.where(kk == mid - 1 + 2 * (nn & 1), 0.25, 0.0)).astype(jnp.bfloat16)
+    for copy in moved:
+        copy.wait()
     block_count = moves_ref.shape[3]
     table_ref[...] = jnp.zeros(table_ref.shape, jnp.int32)
     table_ref[:bands, :block_count] = moves_ref[0, 1]
     table_ref[bands : 2 * bands, :block_count] = moves_ref[0, 0]
     table_ref[2 * bands : 3 * bands, :block_count] = scores_ref[0]
     table_ref[...] = pltpu.roll(table_ref[...], SIDE, 1)
-    for acc in (val_a, val_b):
-        def clear(t, carry, acc=acc):
-            acc[t] = jnp.zeros(acc.shape[1:], jnp.float32)
-            return carry
-        lax.fori_loop(0, acc.shape[0], clear, 0)
-
-    r = lax.broadcasted_iota(jnp.int32, (grid_rows, low_rows), 0)
-    k = lax.broadcasted_iota(jnp.int32, (grid_rows, low_rows), 1)
-    own = r // 2
-    near = jnp.clip(own - 1 + 2 * (r % 2), 0, low_rows - 1)
-    select = jnp.concatenate([(k == own).astype(jnp.float32), (k == near).astype(jnp.float32)], axis=0)
-    picked = jnp.dot(select.astype(jnp.bfloat16), frame_ref[0], preferred_element_type=jnp.float32)
-    rows_ref[:, LANES : LANES + low_cols] = picked.astype(jnp.bfloat16)
-    rows_ref[:, :LANES] = jnp.broadcast_to(picked[:, :1], (2 * grid_rows, LANES)).astype(jnp.bfloat16)
-    rows_ref[:, LANES + low_cols :] = jnp.broadcast_to(
-        picked[:, low_cols - 1 :], (2 * grid_rows, LANES)
-    ).astype(jnp.bfloat16)
-    kk = lax.broadcasted_iota(jnp.int32, (3 * LANES, 2 * LANES), 0)
-    nn = lax.broadcasted_iota(jnp.int32, (3 * LANES, 2 * LANES), 1)
-    mid = nn // 2 + LANES
-    spread = jnp.where(kk == mid, 0.75, jnp.where(kk == mid - 1 + 2 * (nn % 2), 0.25, 0.0)).astype(jnp.bfloat16)
+    first = rows_ref[:, LANES : 2 * LANES].astype(jnp.float32)[:, :1]
+    last = rows_ref[:, low_cols : LANES + low_cols].astype(jnp.float32)[:, LANES - 1 :]
+    rows_ref[:, :LANES] = jnp.broadcast_to(first, (low_rows, LANES)).astype(jnp.bfloat16)
+    rows_ref[:, LANES + low_cols :] = jnp.broadcast_to(last, (low_rows, LANES)).astype(jnp.bfloat16)
+    line = lax.broadcasted_iota(jnp.int32, (low_rows, 2 * LANES), 0)
     lane = lax.broadcasted_iota(jnp.int32, (BLOCK, LANES), 1)
 
     def low_tile(u, carry):
@@ -72,7 +73,14 @@
             rows_ref[:, pl.ds(pl.multiple_of(u * LANES, LANES), 3 * LANES)], spread,
             preferred_element_type=jnp.float32,
         )
-        up_ref[...] = 0.75 * z[:grid_rows] + 0.25 * z[grid_rows:]
+        above = jnp.where(line == 0, z, pltpu.roll(z, 1, 0))
+        below = jnp.where(line == low_rows - 1, z, pltpu.roll(z, low_rows - 1, 0))
+        even = 0.75 * z + 0.25 * above
+        odd = 0.75 * z + 0.25 * below
+        for half in range(2):
+            cols = slice(half * LANES, (half + 1) * LANES)
+            up_ref[half, pl.ds(0, low_rows, stride=2), :] = even[:, cols]
+            up_ref[half, pl.ds(1, low_rows, stride=2), :] = odd[:, cols]
         for half in range(2):
             for j in range(LANES // BLOCK):
                 for b in range(bands):
@@ -84,7 +92,7 @@
                     tile = place >> 7
                     start = place & (LANES - 1)
                     top = MAX_SHIFT + b * BLOCK + dy
-                    block = up_ref[b * BLOCK : (b + 1) * BLOCK, half * LANES : (half + 1) * LANES]
+                    block = up_ref[half, b * BLOCK : (b + 1) * BLOCK, :]
                     block = pltpu.roll(block, dx & (LANES - 1), 1) * w
                     in_a = (lane >= start) & (lane < start + BLOCK)
                     in_b = lane < start + BLOCK - LANES
@@ -109,13 +117,13 @@
     lax.fori_loop(0, strips, strip, 0)
 
 
-def join_kernel(plan, group_size, map_ref, table_ref, image_ref, prior_ref, *refs):
+def join_kernel(plan, group_size, map_hbm, table_ref, image_ref, prior_ref, *refs):
     count = len(plan)
     bits = len(plan[0][2])
     parts = refs[:count]
     out_ref = refs[count]
     landed = refs[count + 1 : count + 1 + count * bits]
-    gathered, staged, move_x, move_y, weight, counts, send_sem, recv_sem, table_send, table_recv = refs[
+    map_ref, map_sem, gathered, staged, move_x, move_y, weight, counts, send_sem, recv_sem, table_send, table_recv = refs[
         count + 1 + count * bits :
     ]
     strip_rows = out_ref.shape[1]
@@ -128,14 +136,24 @@
     def bit_of(bit):
         return (me // 2**bit) % 2
 
-    def partner(bit):
-        other = me + 2**bit - 2 * 2**bit * bit_of(bit)
+    groups = [list(range(3, bits)), [1, 2], [0]]
+    groups = [[bit for bit in group if bit < bits] for group in groups]
+    peers = [[sum(2**bit for n, bit in enumerate(g) if d >> n & 1) for d in range(1, 2 ** len(g))] for g in groups]
+
+    def partner(delta):
+        other = me
+        for bit in range(bits):
+            if delta >> bit & 1:
+                other = other + 2**bit - 2 * 2**bit * bit_of(bit)
         return (other // group_size, other % group_size)
 
+    map_copy = pltpu.make_async_copy(map_hbm, map_ref, map_sem)
+    map_copy.start()
     barrier = pltpu.get_barrier_semaphore()
-    for bit in range(bits):
-        pl.semaphore_signal(barrier, inc=1, device_id=partner(bit), device_id_type=MESH)
-    pl.semaphore_wait(barrier, bits)
+    greeted = sorted(set(sum(peers, [])) | {2**bit for bit in range(bits)})
+    for delta in greeted:
+        pl.semaphore_signal(barrier, inc=1, device_id=partner(delta), device_id_type=MESH)
+    pl.semaphore_wait(barrier, len(greeted))
 
     def source_of(q, stage):
         return parts[q] if stage == 0 else landed[q * bits + stage - 1]
@@ -149,25 +167,31 @@
             dst_ref=landed[q * bits + stage],
             send_sem=send_sem.at[q, stage],
             recv_sem=recv_sem.at[q, stage],
-            device_id=partner(bit),
+            device_id=partner(2**bit),
             device_id_type=MESH,
         )
 
-    slot = 0
-    for step in range(bits):
-        slot = slot + bit_of(bits - 1 - step) * 2**step
-
-    def table_copy(step):
-        size = 2**step
+    slot, scale, sizes = 0, 1, []
+    for group in groups:
+        sizes.append(scale)
+        for bit in group:
+            slot = slot + bit_of(bit) * scale
+            scale = 2 * scale
+
+    def table_copies_of(step):
+        size = sizes[step]
         window = pl.ds(slot // size * size, size)
-        return pltpu.make_async_remote_copy(
-            src_ref=table_ref if step == 0 else gathered.at[window],
-            dst_ref=gathered.at[slot] if step == 0 else gathered.at[window],
-            send_sem=table_send.at[step],
-            recv_sem=table_recv.at[step],
-            device_id=partner(bits - 1 - step),
-            device_id_type=MESH,
-        )
+        return [
+            pltpu.make_async_remote_copy(
+                src_ref=table_ref if step == 0 else gathered.at[window],
+                dst_ref=gathered.at[slot] if step == 0 else gathered.at[window],
+                send_sem=table_send.at[delta],
+                recv_sem=table_recv.at[delta],
+                device_id=partner(delta),
+                device_id_type=MESH,
+            )
+            for delta in peers[step]
+        ]
 
     def turn_tables():
         for f in range(devices):
@@ -202,13 +226,23 @@
         lax.fori_loop(first, last, tile, 0)
 
     copies = {}
-    table_copies = [table_copy(step) for step in range(bits)]
-    table_copies[0].start()
+    table_copies = [table_copies_of(step) for step in range(len(groups))]
+    for copy in table_copies[0]:
+        copy.start()
     for q in range(count):
         copies[q, 0] = copy_of(q, 0)
         copies[q, 0].start()
     gathered[slot] = table_ref[...]
-    count_slots = list(range(bits, 2 * bits - 1))
+
+    def next_tables(step):
+        for copy in table_copies[step]:
+            copy.wait_recv()
+        if step + 1 < len(groups):
+            for copy in table_copies[step + 1]:
+                copy.start()
+
+    next_tables(0)
+    count_slots = list(range(2, 2 * bits - 2))
     for stage in range(bits):
         for chunk in range(2):
             for q in range(chunk * count // 2, (chunk + 1) * count // 2):
@@ -222,13 +256,12 @@
                     copies[q, stage + 1] = copy_of(q, stage + 1)
                     copies[q, stage + 1].start()
             at = 2 * stage + chunk
-            step = at - 1
-            if 0 <= step < bits:
-                table_copies[step].wait_recv()
-                if step + 1 < bits:
-                    table_copies[step + 1].start()
-                else:
-                    turn_tables()
+            if at == 1:
+                next_tables(1)
+            if at == 2:
+                next_tables(2)
+                map_copy.wait()
+                turn_tables()
             if at in count_slots:
                 n = count_slots.index(at)
                 count_tiles(tiles * n // len(count_slots), tiles * (n + 1) // len(count_slots))
@@ -240,7 +273,7 @@
             cols = slice(t * LANES, (t + 1) * LANES)
             prior = prior_ref[0, :, cols]
             out_ref[0, :, cols] = (weighted + prior * image_ref[0, :, cols]) / (counts[t, :strip_rows, :] + prior)
-    for copy in list(copies.values()) + table_copies:
+    for copy in list(copies.values()) + sum(table_copies, []):
         copy.wait_send()
 
 
@@ -252,7 +285,7 @@
     plan = part_plan(strips, tiles)
     bits = len(plan[0][2])
     vmem = pl.BlockSpec(memory_space=pltpu.VMEM)
-    smem = pl.BlockSpec(memory_space=pltpu.SMEM)
+    hbm = pl.BlockSpec(memory_space=pltpu.HBM)
     sizes = [(high - low) * strip_rows for low, high, _ in plan]
     acc = pltpu.VMEM((tiles + 3, 2 * low_rows + 2 * MAX_SHIFT, LANES), jnp.float32)
     bands = motion.shape[2]
@@ -263,15 +296,22 @@
         functools.partial(splat_kernel, plan, strip_rows),
         out_shape=[jax.ShapeDtypeStruct((table_rows, width), jnp.int32)]
         + [jax.ShapeDtypeStruct((strips, size, LANES), jnp.float32) for size in sizes],
-        in_specs=[smem, smem, smem, vmem, vmem, vmem],
+        in_specs=[hbm] * 4,
         out_specs=[vmem] * (1 + len(plan)),
         scratch_shapes=[
-            pltpu.VMEM((4 * low_rows, low_cols + 2 * LANES), jnp.bfloat16),
-            pltpu.VMEM((2 * low_rows, 2 * LANES), jnp.float32),
+            pltpu.SMEM(strip_map.shape, jnp.int32),
+            pltpu.SMEM(motion.shape, jnp.int32),
+            pltpu.SMEM(weights.shape, jnp.int32),
+            pltpu.VMEM(motion.shape, jnp.int32),
+            pltpu.VMEM(weights.shape, jnp.int32),
+            pltpu.VMEM((low_rows, low_cols + 2 * LANES), jnp.bfloat16),
+            pltpu.VMEM((2, 2 * low_rows, LANES), jnp.float32),
             acc, acc,
+            pltpu.SemaphoreType.DMA((6,)),
         ],
+        compiler_params=pltpu.CompilerParams(vmem_limit_bytes=20 * 2**20),
         name="splat",
-    )(strip_map, motion, weights, frames, motion, weights)
+    )(strip_map, motion, weights, frames)
     landed = [
         pltpu.VMEM((strips >> (stage + 1), size, LANES), jnp.float32)
         for size in sizes for stage in range(bits)
@@ -279,9 +319,11 @@
     return pl.pallas_call(
         functools.partial(join_kernel, plan, group_size),
         out_shape=jax.ShapeDtypeStruct(prior_image.shape, jnp.float32),
-        in_specs=[smem] + [vmem] * (3 + len(plan)),
+        in_specs=[hbm] + [vmem] * (3 + len(plan)),
         out_specs=vmem,
         scratch_shapes=landed + [
+            pltpu.SMEM(strip_map.shape, jnp.int32),
+            pltpu.SemaphoreType.DMA(()),
             pltpu.VMEM((strips, table_rows, width), jnp.int32),
             pltpu.VMEM((3, blocks, width), jnp.int32),
             pltpu.VMEM((width, blocks), jnp.int32),
@@ -290,10 +332,12 @@
             pltpu.VMEM((tiles, 8, LANES), jnp.float32),
             pltpu.SemaphoreType.DMA((len(plan), bits)),
             pltpu.SemaphoreType.DMA((len(plan), bits)),
-            pltpu.SemaphoreType.DMA((bits,)),
-            pltpu.SemaphoreType.DMA((bits,)),
+            pltpu.SemaphoreType.DMA((strips,)),
+            pltpu.SemaphoreType.DMA((strips,)),
         ],
-        compiler_params=pltpu.CompilerParams(collective_id=0, has_side_effects=True),
+        compiler_params=pltpu.CompilerParams(
+            collective_id=0, has_side_effects=True, vmem_limit_bytes=16 * 2**20
+        ),
         name="join",
     )(strip_map, table, prior_image, prior_weight, *parts)
 

time: 45.1 us -> 40 us (0.89)
  the two profiles are of different devices: /device:TPU:1 before, /device:TPU:0 now
where the time goes in v2:
time: 40 us; the launch traced here: 39.7 us
  Pallas kernels  36.1 us (90%)
  local copies, waits for them, and re-layouts  3.6 us (9%)
    pallas_call x1, Pallas kernels, body(): pl.pallas_call(functools.partial(join_kernel, plan, group_size), out_shap...  27.1 us
    pallas_call x1, Pallas kernels, body(): pl.pallas_call(functools.partial(splat_kernel, plan, strip_rows), out_sha...  8.97 us
    unnamed x13, local copies, waits for them, and re-layouts  3.6 us

profile of v2, /device:TPU:0, one launch (start us, length us, event | category | flops | bytes accessed | tf_op | source)
XLA Modules:
  0.0 39.7 jit_solution(14245322261245739222)
XLA Ops:
  0.0 0.0 copy-start
  0.0 0.9 %copy-done = bf16[1,64,1920]{2,1,0:T(8,128)(2,1)S(1)} copy-done((bf16[1,64,1920]{2,1,0:T(8,128)(2,1)S(1)}, bf16[1,64,1920]{2,1,0:T(8,128)(2,1)}, u32[]{:S(2)}) %copy-start) | copy-done | bytes 245784
  0.9 0.0 copy-start.3
  0.9 0.7 %copy-done.3 = s32[1,2,4,120]{3,2,1,0:T(4,128)S(1)} copy-done((s32[1,2,4,120]{3,2,1,0:T(4,128)S(1)}, s32[1,2,4,120]{3,2,1,0:T(4,128)}, u32[]{:S(2)}) %copy-start.3) | copy-done | bytes 3864
  1.6 0.0 copy-start.4
  1.6 0.7 %copy-done.4 = s32[1,4,120]{2,1,0:T(4,128)S(1)} copy-done((s32[1,4,120]{2,1,0:T(4,128)S(1)}, s32[1,4,120]{2,1,0:T(4,128)}, u32[]{:S(2)}) %copy-start.4) | copy-done | bytes 1944
  2.3 0.0 copy-start.5
  2.3 0.7 %copy-done.5 = s32[32]{0:T(128)S(1)} copy-done((s32[32]{0:T(128)S(1)}, s32[32]{0:T(128)}, u32[]{:S(2)}) %copy-start.5) | copy-done | bytes 152
  3.0 0.0 copy-start.1
  3.0 0.0 copy-start.2
  3.0 9.0 %splat.1 = (s32[16,128]{1,0:T(8,128)S(1)}, f32[32,24,128]{2,1,0:T(8,128)S(1)}, f32[32,24,128]{2,1,0:T(8,128)S(1)}, f32[32,24,128]{2,1,0:T(8,128)S(1)}, f32[32,16...) custom-call(s32[32]{0:T(128)S(1)} %copy-done.5, s32[1,2,4,120]{3,2,1,0:T(4,128)S(1)} %copy-done.3, ...), custom_call_target="tpu_custom_call" | custom-call | tf_op jit(solution)/shard_map/splat/pallas_call | solution.py:295
  11.9 0.0 copy-done.1
  12.0 0.0 copy-done.2
  12.0 27.1 %join.1 = f32[1,4,3840]{2,1,0:T(4,128)S(1)} custom-call(s32[32]{0:T(128)S(1)} %copy-done.5, s32[16,128]{1,0:T(8,128)S(1)} %get-tuple-element.12.table_ref, f32[1,4,3840]{2,1,0:T(4,128)S(1)} %copy-done.1, f32[1,4,3840]{2,1,0:T(4,128)S(1)} %copy-done.2, f32[32,24,128]{2,1,0:T(8,128)S(1)} %get-tuple-element.13.refs_0_, ...), custom_call_target="tpu_custom_call" | custom-call | tf_op jit(solution)/shard_map/join/pallas_call | solution.py:319
  39.1 0.6 %copy.8 = f32[1,4,3840]{2,1,0:T(4,128)} copy(f32[1,4,3840]{2,1,0:T(4,128)S(1)} %join.1) | data formatting | bytes 122880
Async XLA Ops:
  0.0 0.9 %copy-start = (bf16[1,64,1920]{2,1,0:T(8,128)(2,1)S(1)}, bf16[1,64,1920]{2,1,0:T(8,128)(2,1)}, u32[]{:S(2)}) copy-start(bf16[1,64,1920]{2,1,0:T(8,128)(2,1)} %frame_hbm.1) | copy-start | bytes 737284
  0.9 0.7 %copy-start.3 = (s32[1,2,4,120]{3,2,1,0:T(4,128)S(1)}, s32[1,2,4,120]{3,2,1,0:T(4,128)}, u32[]{:S(2)}) copy-start(s32[1,2,4,120]{3,2,1,0:T(4,128)} %motion_hbm.1) | copy-start | bytes 11524
  1.6 0.7 %copy-start.4 = (s32[1,4,120]{2,1,0:T(4,128)S(1)}, s32[1,4,120]{2,1,0:T(4,128)}, u32[]{:S(2)}) copy-start(s32[1,4,120]{2,1,0:T(4,128)} %weight_hbm.1) | copy-start | bytes 5764
  2.3 0.7 %copy-start.5 = (s32[32]{0:T(128)S(1)}, s32[32]{0:T(128)}, u32[]{:S(2)}) copy-start(s32[32]{0:T(128)} %map_hbm.3) | copy-start | bytes 388
  3.0 9.0 %copy-start.1 = (f32[1,4,3840]{2,1,0:T(4,128)S(1)}, f32[1,4,3840]{2,1,0:T(4,128)}, u32[]{:S(2)}) copy-start(f32[1,4,3840]{2,1,0:T(4,128)} %image_ref.1) | copy-start | bytes 184324
  3.0 9.0 %copy-start.2 = (f32[1,4,3840]{2,1,0:T(4,128)S(1)}, f32[1,4,3840]{2,1,0:T(4,128)}, u32[]{:S(2)}) copy-start(f32[1,4,3840]{2,1,0:T(4,128)} %prior_ref.1) | copy-start | bytes 184324

commit v3 on v2

--- a/solution.py
+++ b/solution.py
@@ -241,8 +241,7 @@
             for copy in table_copies[step + 1]:
                 copy.start()
 
-    next_tables(0)
-    count_slots = list(range(2, 2 * bits - 2))
+    count_slots = list(range(3, 2 * bits - 1))
     for stage in range(bits):
         for chunk in range(2):
             for q in range(chunk * count // 2, (chunk + 1) * count // 2):
@@ -257,8 +256,10 @@
                     copies[q, stage + 1].start()
             at = 2 * stage + chunk
             if at == 1:
+                next_tables(0)
+            if at == 2:
                 next_tables(1)
-            if at == 2:
+            if at == 3:
                 next_tables(2)
                 map_copy.wait()
                 turn_tables()
@@ -311,7 +312,7 @@
         ],
         compiler_params=pltpu.CompilerParams(vmem_limit_bytes=20 * 2**20),
         name="splat",
-    )(strip_map, motion, weights, frames)
+    )(*(pltpu.with_memory_space_constraint(x, pltpu.HBM) for x in (strip_map, motion, weights, frames)))
     landed = [
         pltpu.VMEM((strips >> (stage + 1), size, LANES), jnp.float32)
         for size in sizes for stage in range(bits)
@@ -339,7 +340,7 @@
             collective_id=0, has_side_effects=True, vmem_limit_bytes=16 * 2**20
         ),
         name="join",
-    )(strip_map, table, prior_image, prior_weight, *parts)
+    )(pltpu.with_memory_space_constraint(strip_map, pltpu.HBM), table, prior_image, prior_weight, *parts)
 
 
 def solution(mesh):

time: 40 us -> 35.7 us (0.89)
  local copies, waits for them, and re-layouts: 3.6 us -> 0.63 us
  Pallas kernels: 36.1 us -> 34.9 us
    unnamed x13 -> x5, local copies, waits for them, and re-layouts: 3.6 us -> 0.63 us
    pallas_call x1, Pallas kernels: 27.1 us -> 25.8 us  [body(): pl.pallas_call(functools.partial(join_kernel, plan, group_size), out_shap...]
where the time goes in v3:
time: 35.7 us; the launch traced here: 35.5 us
  Pallas kernels  34.9 us (98%)
  local copies, waits for them, and re-layouts  0.63 us (2%)
    pallas_call x1, Pallas kernels, body(): pl.pallas_call(functools.partial(join_kernel, plan, group_size), out_shap...  25.8 us
    pallas_call x1, Pallas kernels, body(): pl.pallas_call(functools.partial(splat_kernel, plan, strip_rows), out_sha...  9.1 us

profile of v3, /device:TPU:0, one launch (start us, length us, event | category | flops | bytes accessed | tf_op | source)
XLA Modules:
  0.0 35.5 jit_solution(3487307667165973067)
XLA Ops:
  0.0 0.0 copy-start.1
  0.0 0.0 copy-start
  0.0 9.1 %splat.1 = (s32[16,128]{1,0:T(8,128)S(1)}, f32[32,24,128]{2,1,0:T(8,128)S(1)}, f32[32,24,128]{2,1,0:T(8,128)S(1)}, f32[32,24,128]{2,1,0:T(8,128)S(1)}, f32[32,16...) custom-call(s32[32]{0:T(128)} %map_hbm.3, s32[1,2,4,120]{3,2,1,0:T(4,128)} %motion_hbm.1, ...), custom_call_target="tpu_custom_call" | custom-call | tf_op jit(solution)/shard_map/splat/pallas_call | solution.py:296
  9.1 0.0 copy-done.1
  9.1 0.0 copy-done
  9.1 25.8 %join.1 = f32[1,4,3840]{2,1,0:T(4,128)S(1)} custom-call(s32[32]{0:T(128)} %map_hbm.3, s32[16,128]{1,0:T(8,128)S(1)} %get-tuple-element.12.table_ref, f32[1,4,3840]{2,1,0:T(4,128)S(1)} %copy-done, f32[1,4,3840]{2,1,0:T(4,128)S(1)} %copy-done.1, f32[32,24,128]{2,1,0:T(8,128)S(1)} %get-tuple-element.13.refs_0_, f32[32,24,128]{2,1,0:T(8,128)S(1)} %get-tuple-element.14.refs_1_, ...), custom_call_target="tpu_custom_call" | custom-call | tf_op jit(solution)/shard_map/join/pallas_call | solution.py:320
  34.9 0.6 %copy.8 = f32[1,4,3840]{2,1,0:T(4,128)} copy(f32[1,4,3840]{2,1,0:T(4,128)S(1)} %join.1) | data formatting | bytes 122880
Async XLA Ops:
  0.0 9.1 %copy-start.1 = (f32[1,4,3840]{2,1,0:T(4,128)S(1)}, f32[1,4,3840]{2,1,0:T(4,128)}, u32[]{:S(2)}) copy-start(f32[1,4,3840]{2,1,0:T(4,128)} %prior_ref.1) | copy-start | bytes 184324
  0.0 9.1 %copy-start = (f32[1,4,3840]{2,1,0:T(4,128)S(1)}, f32[1,4,3840]{2,1,0:T(4,128)}, u32[]{:S(2)}) copy-start(f32[1,4,3840]{2,1,0:T(4,128)} %image_ref.1) | copy-start | bytes 184324

commit v4 on v3

--- a/solution.py
+++ b/solution.py
@@ -241,7 +241,7 @@
             for copy in table_copies[step + 1]:
                 copy.start()
 
-    count_slots = list(range(3, 2 * bits - 1))
+    count_slots = list(range(4, 2 * bits - 1))
     for stage in range(bits):
         for chunk in range(2):
             for q in range(chunk * count // 2, (chunk + 1) * count // 2):
@@ -257,9 +257,9 @@
             at = 2 * stage + chunk
             if at == 1:
                 next_tables(0)
-            if at == 2:
+            if at == 3:
                 next_tables(1)
-            if at == 3:
+            if at == 4:
                 next_tables(2)
                 map_copy.wait()
                 turn_tables()

time: 35.7 us -> 35 us (0.980)
  Pallas kernels: 34.9 us -> 34.2 us
    pallas_call x1, Pallas kernels: 25.8 us -> 25.1 us  [body(): pl.pallas_call(functools.partial(join_kernel, plan, group_size), out_shap...]
where the time goes in v4:
time: 35 us; the launch traced here: 34.9 us
  Pallas kernels  34.2 us (98%)
  local copies, waits for them, and re-layouts  0.63 us (2%)
    pallas_call x1, Pallas kernels, body(): pl.pallas_call(functools.partial(join_kernel, plan, group_size), out_shap...  25.1 us
    pallas_call x1, Pallas kernels, body(): pl.pallas_call(functools.partial(splat_kernel, plan, strip_rows), out_sha...  9.1 us

profile of v4, /device:TPU:0, one launch (start us, length us, event | category | flops | bytes accessed | tf_op | source)
XLA Modules:
  0.0 34.9 jit_solution(5113943834518122938)
XLA Ops:
  0.0 0.0 copy-start.1
  0.0 0.0 copy-start
  0.0 9.1 %splat.1 = (s32[16,128]{1,0:T(8,128)S(1)}, f32[32,24,128]{2,1,0:T(8,128)S(1)}, f32[32,24,128]{2,1,0:T(8,128)S(1)}, f32[32,24,128]{2,1,0:T(8,128)S(1)}, f32[32,16...) custom-call(s32[32]{0:T(128)} %map_hbm.3, s32[1,2,4,120]{3,2,1,0:T(4,128)} %motion_hbm.1, ...), custom_call_target="tpu_custom_call" | custom-call | tf_op jit(solution)/shard_map/splat/pallas_call | solution.py:296
  9.1 0.0 copy-done.1
  9.1 0.0 copy-done
  9.1 25.1 %join.1 = f32[1,4,3840]{2,1,0:T(4,128)S(1)} custom-call(s32[32]{0:T(128)} %map_hbm.3, s32[16,128]{1,0:T(8,128)S(1)} %get-tuple-element.12.table_ref, f32[1,4,3840]{2,1,0:T(4,128)S(1)} %copy-done, f32[1,4,3840]{2,1,0:T(4,128)S(1)} %copy-done.1, f32[32,24,128]{2,1,0:T(8,128)S(1)} %get-tuple-element.13.refs_0_, f32[32,24,128]{2,1,0:T(8,128)S(1)} %get-tuple-element.14.refs_1_, ...), custom_call_target="tpu_custom_call" | custom-call | tf_op jit(solution)/shard_map/join/pallas_call | solution.py:320
  34.2 0.6 %copy.8 = f32[1,4,3840]{2,1,0:T(4,128)} copy(f32[1,4,3840]{2,1,0:T(4,128)S(1)} %join.1) | data formatting | bytes 122880
Async XLA Ops:
  0.0 9.1 %copy-start.1 = (f32[1,4,3840]{2,1,0:T(4,128)S(1)}, f32[1,4,3840]{2,1,0:T(4,128)}, u32[]{:S(2)}) copy-start(f32[1,4,3840]{2,1,0:T(4,128)} %prior_ref.1) | copy-start | bytes 184324
  0.0 9.1 %copy-start = (f32[1,4,3840]{2,1,0:T(4,128)S(1)}, f32[1,4,3840]{2,1,0:T(4,128)}, u32[]{:S(2)}) copy-start(f32[1,4,3840]{2,1,0:T(4,128)} %image_ref.1) | copy-start | bytes 184324
